TPU v7x, 32 devices: a whole 2x2x4 slice. The times are simulated.
32 devices in a mesh: row: 4 (over y, core), col: 8 (over z, x).
Axes of the slice: x: 2, y: 2, z: 4, core: 2. Of those that a mesh axis runs over, the one named last changes fastest.
Arguments:
- matrix: float32 [16384, 16384], P('row', 'col'), as said below
Outputs:
- updated: float32 [16384, 16384], P('row', 'col')
- reflectors: float32 [1, 16384, 256], P(None, ('row', 'col'))
- products: float32 [1, 16384, 256], P(None, ('row', 'col'))
Inputs may be any that keep to these rules, and one draw needn't show every extreme that they name: `matrix`: symmetric.
All inputs are finite; a program needn't handle non-finite values.
Results may differ from a plain program's by a relative error of at most 0.0003.
Values sent between devices are 32-bit elements; how exact they have to be, the bound alone decides.
A program may use at most 192 MiB of HBM per device.

v0:
```python
import jax
import jax.numpy as jnp
from jax import lax
from jax.sharding import PartitionSpec as P

NB = 256
leaf_width = 16


def spread(value, axis, source):
    kept = jnp.where(lax.axis_index(axis) == source, value, 0).astype(value.dtype)
    return lax.psum(kept, axis)


def matmul(left, right):
    return jnp.dot(left, right, precision=lax.Precision.HIGHEST, preferred_element_type=jnp.float32)


def lu_signed(square):
    order_n = square.shape[0]
    width = min(leaf_width, order_n)
    all_ids = jnp.arange(order_n)
    panel_ids = jnp.arange(width)
    work_mat = square
    sign_vec = jnp.zeros((order_n,), jnp.float32)
    for first in range(0, order_n, width):
        panel = work_mat[:, first : first + width]

        def leaf_step(local_idx, state, first=first):
            panel, sign_vec = state
            pivot_idx = first + local_idx
            column = lax.dynamic_slice_in_dim(panel, local_idx, 1, 1)[:, 0]
            raw_pivot = column[pivot_idx]
            sign_now = jnp.where(raw_pivot >= 0, 1.0, -1.0).astype(jnp.float32)
            pivot_val = raw_pivot + sign_now
            lower_col = jnp.where(all_ids > pivot_idx, column / pivot_val, 0.0)
            upper_row = jnp.where(panel_ids > local_idx, panel[pivot_idx, :], 0.0)
            panel = panel - lower_col[:, None] * upper_row[None, :]
            kept = jnp.where(
                all_ids > pivot_idx, lower_col, jnp.where(all_ids == pivot_idx, pivot_val, column)
            )
            panel = lax.dynamic_update_slice_in_dim(panel, kept[:, None], local_idx, 1)
            sign_vec = sign_vec.at[pivot_idx].set(sign_now)
            return (panel, sign_vec)

        panel, sign_vec = lax.fori_loop(0, width, leaf_step, (panel, sign_vec))
        work_mat = work_mat.at[:, first : first + width].set(panel)
        after = first + width
        if after < order_n:
            diag_lower = jnp.tril(panel[first:after], -1) + jnp.eye(width, dtype=jnp.float32)
            upper_right = jax.scipy.linalg.solve_triangular(
                diag_lower, work_mat[first:after, after:], lower=True, unit_diagonal=True
            )
            trailing = work_mat[after:, after:] - matmul(panel[after:], upper_right)
            work_mat = work_mat.at[first:after, after:].set(upper_right)
            work_mat = work_mat.at[after:, after:].set(trailing)
    unit_lower = jnp.tril(work_mat, -1) + jnp.eye(order_n, dtype=jnp.float32)
    return (unit_lower, jnp.triu(work_mat), sign_vec)


def body(matrix):
    row_count, col_count = matrix.shape
    row_index = lax.axis_index("row")
    col_index = lax.axis_index("col")
    col_devices = lax.axis_size("col")
    share_rows = row_count // col_devices
    row_ids = row_index * row_count + jnp.arange(row_count)
    owner_row = col_index * col_count // row_count
    owner_offset = col_index * col_count % row_count
    current = matrix
    row_start = NB
    panel_cols = lax.slice_in_dim(current, 0, NB, axis=1)
    panel_cols = spread(panel_cols, "col", 0)
    panel_cols = jnp.where((row_ids >= row_start)[:, None], panel_cols, 0.0)
    gram_sum = lax.psum(matmul(panel_cols.T, panel_cols), "row")
    chol_low = jnp.linalg.cholesky(gram_sum)
    q_basis = jax.scipy.linalg.solve_triangular(chol_low, panel_cols.T, lower=True).T
    top_block = spread(q_basis[row_start : row_start + NB], "row", 0)
    unit_lower, upper_tri, sign_diag = lu_signed(top_block)
    solved = jax.scipy.linalg.solve_triangular(upper_tri.T, q_basis.T, lower=True).T
    rel_pos = row_ids - row_start
    in_top = (rel_pos >= 0) & (rel_pos < NB)
    lower_rows = jnp.take(unit_lower, jnp.clip(rel_pos, 0, NB - 1), axis=0)
    refl = jnp.where(in_top[:, None], lower_rows, jnp.where((rel_pos < 0)[:, None], 0.0, solved))
    scaled = upper_tri * sign_diag[None, :]
    t_factor = jax.scipy.linalg.solve_triangular(
        unit_lower, scaled.T, lower=True, unit_diagonal=True
    ).T
    own_slice = lax.dynamic_slice_in_dim(refl, owner_offset, col_count, 0)
    refl_cols = spread(own_slice, "row", owner_row)
    x_rows = lax.psum(matmul(current, matmul(refl_cols, t_factor)), "col")
    inner_prod = lax.psum(matmul(refl.T, x_rows), "row")
    correction = matmul(t_factor.T, inner_prod)
    w_rows = x_rows - 0.5 * matmul(refl, correction)
    x_cols = lax.psum(matmul(current.T, matmul(refl, t_factor)), "row")
    w_cols = x_cols - 0.5 * matmul(refl_cols, correction)
    left_pair = jnp.concatenate([refl, w_rows], axis=1)
    right_pair = jnp.concatenate([w_cols, refl_cols], axis=1)
    current = current - matmul(left_pair, right_pair.T)
    all_refl = [lax.dynamic_slice_in_dim(refl, col_index * share_rows, share_rows, 0)]
    all_prod = [lax.dynamic_slice_in_dim(w_rows, col_index * share_rows, share_rows, 0)]
    return (current, jnp.stack(all_refl), jnp.stack(all_prod))


def solution(mesh):
    return jax.shard_map(
        body,
        mesh=mesh,
        in_specs=(P("row", "col"),),
        out_specs=(P("row", "col"), P(None, ("row", "col"), None), P(None, ("row", "col"), None)),
        check_vma=False,
    )
```

profile of v0, /device:TPU:0, one launch (start us, length us, event | category | flops | bytes accessed | tf_op | source)
XLA Modules:
  0.0 1536.2 jit_solution(7830137127578075882)
XLA Ops:
  7.2 4.5 slice_select_fusion
  12.6 158.8 %all-reduce.9.cloned.1.call-done = f32[4096,256]{1,0:T(8,128)} async-done(((f32[4096,256]{1,0:T(8,128)}), f32[4096,256]{1,0:T(8,128)}) %all-reduce.9.cloned.1.call-update) | async-done | bytes 4194320 | tf_op jit(solution)/shard_map/psum | solution.py:12
  171.4 12.2 fusion.89
  183.8 3.9 select_bitcast_fusion
  187.8 27.3 %all-reduce.11.cloned.1.call-done = f32[256,256]{0,1:T(8,128)} async-done(((f32[256,256]{0,1:T(8,128)}), f32[256,256]{0,1:T(8,128)}) %all-reduce.11.cloned.1.call-update) | async-done | bytes 262160 | tf_op jit(solution)/shard_map/psum | solution.py:75
  217.1 11.7 cholesky.50
  228.9 9.8 custom-call.78
  239.2 11.7 cholesky.105
  253.1 4.0 while.404
  257.0 19.9 %custom-call.96 = f32[2,128,128]{1,2,0:T(8,128)S(1)} custom-call(f32[2,128,128]{2,1,0:T(8,128)S(1)} %get-tuple-element.3807), custom_call_target="InvertDiagBlocksLowerTriangular" | custom-call | tf_op jit(solution)/shard_map/jit(_solve_triangular)/triangular_solve | solution.py:77
  276.9 3.7 fusion.92
  280.6 4.8 convolution_subtract_fusion.2
  287.2 3.5 fusion.110
  303.7 21.8 %all-reduce.13.cloned.1.call-done = f32[256,256]{1,0:T(8,128)} async-done(((f32[256,256]{1,0:T(8,128)}), f32[256,256]{1,0:T(8,128)}) %all-reduce.13.cloned.1.call-update) | async-done | bytes 262160 | tf_op jit(solution)/shard_map/psum | solution.py:12
  326.5 37.1 %while.388 = (s32[]{:T(128)}, f32[256,16]{0,1:T(8,128)S(1)}, f32[256]{0:T(256)S(1)}, s32[]{:T(128)}, s32[]{:T(128)}, /*index=5*/s32[]{:T(128)}, s32[]{:T(128)}, f32[]{:T(128)}, f32[]{:T(128)}, f32[]{:T(128)}) while((s32[]{:T(128)}, f32[256,16]{0,1:T(8,128)S(1)}, f32[256]{0:T(256)S(1)}, s32[]{:T(128)}, s32[]{:T(128)}, ...), condition=%wide.region_9.11_spmd.clone.clone, body=%wide.region_8.10_spmd.clone.clone.sunk | while | flops 9771 | bytes 75169 | solution.py:46
  368.2 2.8 dynamic-slice_select_fusion.1
  372.4 3.4 scatter.220
  375.9 2.4 scatter.221
  379.3 37.1 %while.389 = (s32[]{:T(128)}, f32[256,16]{0,1:T(8,128)S(1)}, f32[256]{0:T(256)S(1)}, s32[]{:T(128)}, s32[]{:T(128)}, /*index=5*/s32[]{:T(128)}, s32[]{:T(128)}, ...) while((s32[]{:T(128)}, f32[256,16]{0,1:T(8,128)S(1)}, ...), condition=%wide.region_13.15_spmd.clone.clone, body=%wide.region_12.14_spmd.clone.clone.sunk | while | flops 9775 | bytes 74215 | solution.py:46
  423.8 2.3 scatter.225
  426.0 2.4 scatter.226
  429.5 37.1 %while.390 = (s32[]{:T(128)}, f32[256,16]{0,1:T(8,128)S(1)}, f32[256]{0:T(256)S(1)}, s32[]{:T(128)}, s32[]{:T(128)}, /*index=5*/s32[]{:T(128)}, s32[]{:T(128)}, ...) while((s32[]{:T(128)}, f32[256,16]{0,1:T(8,128)S(1)}, ...), condition=%wide.region_16.18_spmd.clone.clone, body=%wide.region_15.17_spmd.clone.clone.sunk | while | flops 9775 | bytes 74215 | solution.py:46
  473.8 2.3 scatter.230
  476.1 2.3 scatter.231
  479.5 37.1 %while.391 = (s32[]{:T(128)}, f32[256,16]{0,1:T(8,128)S(1)}, f32[256]{0:T(256)S(1)}, s32[]{:T(128)}, s32[]{:T(128)}, /*index=5*/s32[]{:T(128)}, s32[]{:T(128)}, ...) while((s32[]{:T(128)}, f32[256,16]{0,1:T(8,128)S(1)}, ...), condition=%wide.region_19.21_spmd.clone.clone, body=%wide.region_18.20_spmd.clone.clone.sunk | while | flops 9775 | bytes 74215 | solution.py:46
  523.8 2.2 scatter.235
  526.0 2.3 scatter.237
  529.4 37.1 %while.392 = (s32[]{:T(128)}, f32[256,16]{0,1:T(8,128)S(1)}, f32[256]{0:T(256)S(1)}, s32[]{:T(128)}, s32[]{:T(128)}, /*index=5*/s32[]{:T(128)}, s32[]{:T(128)}, ...) while((s32[]{:T(128)}, f32[256,16]{0,1:T(8,128)S(1)}, ...), condition=%wide.region_22.24_spmd.clone.clone, body=%wide.region_21.23_spmd.clone.clone.sunk | while | flops 9775 | bytes 74215 | solution.py:46
  573.6 2.2 scatter.241
  575.9 2.2 scatter.242
  579.1 37.1 %while.393 = (s32[]{:T(128)}, f32[256,16]{0,1:T(8,128)S(1)}, f32[256]{0:T(256)S(1)}, s32[]{:T(128)}, s32[]{:T(128)}, /*index=5*/s32[]{:T(128)}, s32[]{:T(128)}, ...) while((s32[]{:T(128)}, f32[256,16]{0,1:T(8,128)S(1)}, ...), condition=%wide.region_25.27_spmd.clone.clone, body=%wide.region_24.26_spmd.clone.clone.sunk | while | flops 9775 | bytes 74215 | solution.py:46
  623.5 2.3 scatter.246
  625.7 2.2 scatter.247
  629.0 37.1 %while.394 = (s32[]{:T(128)}, f32[256,16]{0,1:T(8,128)S(1)}, f32[256]{0:T(256)S(1)}, s32[]{:T(128)}, s32[]{:T(128)}, /*index=5*/s32[]{:T(128)}, s32[]{:T(128)}, ...) while((s32[]{:T(128)}, f32[256,16]{0,1:T(8,128)S(1)}, ...), condition=%wide.region_28.30_spmd.clone.clone, body=%wide.region_27.29_spmd.clone.clone.sunk | while | flops 9775 | bytes 74215 | solution.py:46
  673.3 2.4 scatter.251
  675.7 2.1 scatter.252
  678.9 37.1 %while.395 = (s32[]{:T(128)}, f32[256,16]{0,1:T(8,128)S(1)}, f32[256]{0:T(256)S(1)}, s32[]{:T(128)}, s32[]{:T(128)}, /*index=5*/s32[]{:T(128)}, s32[]{:T(128)}, ...) while((s32[]{:T(128)}, f32[256,16]{0,1:T(8,128)S(1)}, ...), condition=%wide.region_31.33_spmd.clone.clone, body=%wide.region_30.32_spmd.clone.clone.sunk | while | flops 9775 | bytes 74215 | solution.py:46
  724.0 37.1 %while.396 = (s32[]{:T(128)}, f32[256,16]{0,1:T(8,128)S(1)}, f32[256]{0:T(256)S(1)}, s32[]{:T(128)}, s32[]{:T(128)}, /*index=5*/s32[]{:T(128)}, s32[]{:T(128)}, ...) while((s32[]{:T(128)}, f32[256,16]{0,1:T(8,128)S(1)}, ...), condition=%wide.region_34.36_spmd.clone.clone, body=%wide.region_33.35_spmd.clone.clone.sunk | while | flops 9775 | bytes 74215 | solution.py:46
  766.7 37.1 %while.397 = (s32[]{:T(128)}, f32[256,16]{0,1:T(8,128)S(1)}, f32[256]{0:T(256)S(1)}, s32[]{:T(128)}, s32[]{:T(128)}, /*index=5*/s32[]{:T(128)}, s32[]{:T(128)}, ...) while((s32[]{:T(128)}, f32[256,16]{0,1:T(8,128)S(1)}, ...), condition=%wide.region_37.39_spmd.clone.clone, body=%wide.region_36.38_spmd.clone.clone.sunk | while | flops 9775 | bytes 74215 | solution.py:46
  809.5 37.1 %while.398 = (s32[]{:T(128)}, f32[256,16]{0,1:T(8,128)S(1)}, f32[256]{0:T(256)S(1)}, s32[]{:T(128)}, s32[]{:T(128)}, /*index=5*/s32[]{:T(128)}, s32[]{:T(128)}, ...) while((s32[]{:T(128)}, f32[256,16]{0,1:T(8,128)S(1)}, ...), condition=%wide.region_40.42_spmd.clone.clone, body=%wide.region_39.41_spmd.clone.clone.sunk | while | flops 9775 | bytes 74215 | solution.py:46
  852.3 37.1 %while.399 = (s32[]{:T(128)}, f32[256,16]{0,1:T(8,128)S(1)}, f32[256]{0:T(256)S(1)}, s32[]{:T(128)}, s32[]{:T(128)}, /*index=5*/s32[]{:T(128)}, s32[]{:T(128)}, ...) while((s32[]{:T(128)}, f32[256,16]{0,1:T(8,128)S(1)}, ...), condition=%wide.region_43.45_spmd.clone.clone, body=%wide.region_42.44_spmd.clone.clone.sunk | while | flops 9775 | bytes 74215 | solution.py:46
  894.9 37.1 %while.400 = (s32[]{:T(128)}, f32[256,16]{0,1:T(8,128)S(1)}, f32[256]{0:T(256)S(1)}, s32[]{:T(128)}, s32[]{:T(128)}, /*index=5*/s32[]{:T(128)}, s32[]{:T(128)}, ...) while((s32[]{:T(128)}, f32[256,16]{0,1:T(8,128)S(1)}, ...), condition=%wide.region_46.48_spmd.clone.clone, body=%wide.region_45.47_spmd.clone.clone.sunk | while | flops 9775 | bytes 74215 | solution.py:46
  937.6 37.1 %while.401 = (s32[]{:T(128)}, f32[256,16]{0,1:T(8,128)S(1)}, f32[256]{0:T(256)S(1)}, s32[]{:T(128)}, s32[]{:T(128)}, /*index=5*/s32[]{:T(128)}, s32[]{:T(128)}, ...) while((s32[]{:T(128)}, f32[256,16]{0,1:T(8,128)S(1)}, ...), condition=%wide.region_49.51_spmd.clone.clone, body=%wide.region_48.50_spmd.clone.clone.sunk | while | flops 9775 | bytes 74215 | solution.py:46
  980.2 37.1 %while.402 = (s32[]{:T(128)}, f32[256,16]{0,1:T(8,128)S(1)}, f32[256]{0:T(256)S(1)}, s32[]{:T(128)}, s32[]{:T(128)}, /*index=5*/s32[]{:T(128)}, s32[]{:T(128)}, ...) while((s32[]{:T(128)}, f32[256,16]{0,1:T(8,128)S(1)}, ...), condition=%wide.region_52.54_spmd.clone.clone, body=%wide.region_51.53_spmd.clone.clone.sunk | while | flops 9775 | bytes 74215 | solution.py:46
  1022.6 37.1 %while.403 = (s32[]{:T(128)}, f32[256,16]{0,1:T(8,128)S(1)}, f32[256]{0:T(256)S(1)}, s32[]{:T(128)}, s32[]{:T(128)}, /*index=5*/s32[]{:T(128)}, s32[]{:T(128)}, ...) while((s32[]{:T(128)}, f32[256,16]{0,1:T(8,128)S(1)}, ...), condition=%wide.region_54.56_spmd.clone.clone, body=%wide.region_53.55_spmd.clone.clone.sunk | while | flops 9775 | bytes 74215 | solution.py:46
  1060.9 16.1 %gather_fusion = f32[4096,256]{1,0:T(8,128)} fusion(f32[256,256]{1,0:T(8,128)S(1)} %get-tuple-element.4059, s32[4096]{0:T(1024)S(1)} %broadcast_clamp_fusion), kind=kCustom, calls=%fused_computation | custom fusion | bytes 8404992 | tf_op jit(solution)/shard_map/jit(_take)/gather | solution.py:83
  1077.0 5.6 copy.109
  1082.6 4.2 while.405
  1086.9 19.9 %custom-call.97 = f32[2,128,128]{1,2,0:T(8,128)S(1)} custom-call(f32[2,128,128]{2,1,0:T(8,128)S(1)} %get-tuple-element.3808), custom_call_target="InvertDiagBlocksLowerTriangular" | custom-call | tf_op jit(solution)/shard_map/jit(_solve_triangular)/triangular_solve | solution.py:80
  1108.8 3.6 convolution_subtract_fusion.1
  1118.9 4.5 while.387
  1123.4 19.7 %custom-call.94 = f32[2,128,128]{1,2,0:T(8,128)S(1)} custom-call(f32[2,128,128]{2,1,0:T(8,128)S(1)} %get-tuple-element.3432), custom_call_target="InvertDiagBlocksLowerTriangular" | custom-call | tf_op jit(solution)/shard_map/jit(_solve_triangular)/triangular_solve | solution.py:86
  1144.1 26.3 %all-reduce.15.cloned.1.call-done = f32[2048,256]{0,1:T(8,128)} async-done(((f32[2048,256]{0,1:T(8,128)}), f32[2048,256]{0,1:T(8,128)}) %all-reduce.15.cloned.1.call-update) | async-done | bytes 2097168 | tf_op jit(solution)/shard_map/psum | solution.py:12
  1170.4 5.0 fusion.101
  1175.4 58.3 %convolution_bitcast_fusion = f32[4096,256]{0,1:T(8,128)} fusion(f32[2048,256]{1,0:T(8,128)S(1)} %fusion.101, f32[4096,2048]{1,0:T(8,128)} %param.159), kind=kOutput, calls=%fused_computation.205 | convolution fusion | flops 25769803776 | bytes 39845888 | tf_op jit(solution)/shard_map/dot_general | solution.py:16
  1233.8 8.5 fusion.99
  1242.3 33.1 %convolution_bitcast_fusion.1 = f32[2048,256]{0,1:T(8,128)} fusion(f32[4096,256]{1,0:T(8,128)S(1)} %fusion.99, f32[4096,2048]{1,0:T(8,128)} %param.159), kind=kOutput, calls=%fused_computation.221 | convolution fusion | flops 25769803776 | bytes 39845888 | tf_op jit(solution)/shard_map/dot_general | solution.py:16
  1275.4 115.0 %all-reduce.17.cloned.1.call-done = f32[4096,256]{0,1:T(8,128)} async-done(((f32[4096,256]{0,1:T(8,128)}), f32[4096,256]{0,1:T(8,128)}) %all-reduce.17.cloned.1.call-update) | async-done | bytes 4194320 | tf_op jit(solution)/shard_map/psum | solution.py:91
  1390.4 7.7 fusion.222
  1400.2 52.7 %all-reduce.19.cloned.1.call-done = (f32[256,256]{1,0:T(8,128)}, f32[2048,256]{0,1:T(8,128)}) async-done(((f32[256,256]{1,0:T(8,128)}, f32[2048,256]{0,1:T(8,128)}), (f32[256,256]{1,0:T(8,128)}, f32[2048,256]{0,1:T(8,128)})) %all-reduce.19.cloned.1.call-update) | async-done | bytes 2359312 | tf_op jit(solution)/shard_map/psum | solution.py:92
  1454.3 8.2 fusion.83
  1462.5 2.0 copy-done.2
  1465.5 3.8 fusion.91
  1469.3 59.8 %convolution_subtract_fusion = f32[4096,2048]{1,0:T(8,128)} fusion(f32[4096,2048]{1,0:T(8,128)} %param.159, f32[4096,256]{0,1:T(8,128)} %copy-done.2, f32[4096,256]{0,1:T(8,128)S(1)} %copy-done.1, f32[2048,256]{0,1:T(8,128)S(1)} %copy-done.5, f32[2048,256]{0,1:T(8,128)S(1)} %fusion.91), kind=kOutput, calls=%fused_computation.199 | convolution fusion | flops 51551141888 | bytes 79691776 | tf_op jit(solution)/shard_map/dot_general | solution.py:16
  (2313 shorter events, 403.3 us)
Async XLA Ops:
  7.2 164.2 %all-reduce.9.cloned.1.call-start = ((), (), s32[]{:S(2)}) async-start(), calls=%async_computation | async-start | bytes 8388608 | tf_op jit(solution)/shard_map/psum | solution.py:12
  11.7 203.3 %all-reduce.11.cloned.1.call-start = ((), (), s32[]{:S(2)}) async-start(), calls=%async_computation.1 | async-start | bytes 524288 | tf_op jit(solution)/shard_map/psum | solution.py:75
  183.6 141.9 %all-reduce.13.cloned.1.call-start = ((), (), s32[]{:S(2)}) async-start(), calls=%async_computation.2 | async-start | bytes 524288 | tf_op jit(solution)/shard_map/psum | solution.py:12
  276.9 3.7 copy-start.7
  287.2 4.9 copy-start.8
  290.7 1.3 copy-start.3
  292.1 11.0 copy-start.9
  293.1 877.3 %all-reduce.15.cloned.1.call-start = ((), (), s32[]{:S(2)}) async-start(), calls=%async_computation.3 | async-start | bytes 4194304 | tf_op jit(solution)/shard_map/psum | solution.py:12
  1106.8 1.9 copy-start.4
  1108.8 5.5 copy-start.6
  1115.3 2.0 copy-start
  1118.8 271.6 %all-reduce.17.cloned.1.call-start = ((), (), s32[]{:S(2)}) async-start(), calls=%async_computation.4 | async-start | bytes 8388608 | tf_op jit(solution)/shard_map/psum | solution.py:91
  1233.8 219.2 %all-reduce.19.cloned.1.call-start = ((), (), s32[]{:S(2)}) async-start(), calls=%async_computation.5 | async-start | bytes 4718592 | tf_op jit(solution)/shard_map/psum | solution.py:92
  1454.3 11.2 copy-start.5
  1462.4 2.0 copy-start.2
  1465.5 3.9 copy-start.1
Sparse Core Ops, SparseCore 0:
  12.2 159.0 all-reduce.8
  183.7 31.2 all-reduce.10
  293.2 32.2 all-reduce.12
  1118.9 51.4 all-reduce.14
  1233.9 156.4 all-reduce.16
  1398.2 54.6 all-reduce.18
where the time goes:
time: 1550 us; the launch traced here: 1540 us
  waiting for transfers between devices  402 us (26%)
  loops' own time  341 us (22%)
  local copies, waits for them, and re-layouts  308 us (20%)
  matrix products  243 us (16%)
  other arithmetic  225 us (15%)
  between operations  16.7 us (1%)
    another operation x16, loops' own time, lu_signed(): panel, sign_vec = lax.fori_loop(0, width, leaf_step, (panel, sign_vec))  341 us
    dot_general x25, matrix products, matmul(): jnp.dot(left, right, precision=lax.Precision.HIGHEST, preferred_element_t...  211 us
    psum x3, waiting for transfers between devices, spread(): return lax.psum(kept, axis)  207 us
    dynamic_slice x256, local copies, waits for them, and re-layouts, leaf_step(): raw_pivot = column[pivot_idx]  150 us
    psum x1, waiting for transfers between devices, body(): x_rows = lax.psum(matmul(current, matmul(refl_cols, t_factor)), 'col')  115 us
    psum x1, waiting for transfers between devices, body(): inner_prod = lax.psum(matmul(refl.T, x_rows), 'row')  52.7 us
    scatter x256, other arithmetic, leaf_step(): sign_vec = sign_vec.at[pivot_idx].set(sign_now)  43.6 us
    another operation x6, other arithmetic, body(): chol_low = jnp.linalg.cholesky(gram_sum)  34 us
  transfers between devices with their start and end apart: 6, of which 6 were waited for; matrix products, arithmetic and copies ran while one was open for 5% of the time, Pallas kernels for 0%

commit v1 on v0

--- a/solution.py
+++ b/solution.py
@@ -88,7 +88,7 @@
     ).T
     own_slice = lax.dynamic_slice_in_dim(refl, owner_offset, col_count, 0)
     refl_cols = spread(own_slice, "row", owner_row)
-    x_rows = lax.psum(matmul(current, matmul(refl_cols, t_factor)), "col")
+    x_rows = jnp.sum(lax.all_gather(matmul(current, matmul(refl_cols, t_factor)), "col"), axis=0)
     inner_prod = lax.psum(matmul(refl.T, x_rows), "row")
     correction = matmul(t_factor.T, inner_prod)
     w_rows = x_rows - 0.5 * matmul(refl, correction)

time: 1550 us -> 2080 us (1.34)
  waiting for transfers between devices: 402 us -> 885 us
  local copies, waits for them, and re-layouts: 308 us -> 338 us
    all_gather x0 -> x1, waiting for transfers between devices: none -> 596 us  [body(): lax.all_gather(matmul(current, matmul(refl_cols, t_factor)), 'col')]
    psum x1 -> x0, waiting for transfers between devices: 115 us -> none  [body(): x_rows = lax.psum(matmul(current, matmul(refl_cols, t_factor)), 'col')]
    unnamed x37 -> x40, local copies, waits for them, and re-layouts: 7.25 us -> 36.3 us
  transfers between devices with their start and end apart: 6 -> 6, of which waited for: 6 -> 6; matrix products, arithmetic and copies ran while one was open for 5% -> 4% of each run, Pallas kernels for 0% -> 0%
where the time goes in v1:
time: 2080 us; the launch traced here: 2070 us
  waiting for transfers between devices  885 us (43%)
  loops' own time  345 us (17%)
  local copies, waits for them, and re-layouts  338 us (16%)
  matrix products  245 us (12%)
  other arithmetic  240 us (12%)
    all_gather x1, waiting for transfers between devices, body(): lax.all_gather(matmul(current, matmul(refl_cols, t_factor)), 'col')  596 us
    another operation x16, loops' own time, lu_signed(): panel, sign_vec = lax.fori_loop(0, width, leaf_step, (panel, sign_vec))  345 us
    dot_general x25, matrix products, matmul(): jnp.dot(left, right, precision=lax.Precision.HIGHEST, preferred_element_t...  212 us
    psum x3, waiting for transfers between devices, spread(): return lax.psum(kept, axis)  208 us
    dynamic_slice x256, local copies, waits for them, and re-layouts, leaf_step(): raw_pivot = column[pivot_idx]  151 us
    psum x1, waiting for transfers between devices, body(): inner_prod = lax.psum(matmul(refl.T, x_rows), 'row')  53.7 us
    scatter x256, other arithmetic, leaf_step(): sign_vec = sign_vec.at[pivot_idx].set(sign_now)  43.5 us
  transfers between devices with their start and end apart: 6, of which 6 were waited for; matrix products, arithmetic and copies ran while one was open for 4% of the time, Pallas kernels for 0%

profile of v1, /device:TPU:0, one launch (start us, length us, event | category | flops | bytes accessed | tf_op | source)
XLA Modules:
  0.0 2070.9 jit_solution(1587561599813993120)
XLA Ops:
  7.2 4.5 slice_select_fusion
  12.6 158.8 %all-reduce.8.cloned.1.call-done = f32[4096,256]{1,0:T(8,128)} async-done(((f32[4096,256]{1,0:T(8,128)}), f32[4096,256]{1,0:T(8,128)}) %all-reduce.8.cloned.1.call-update) | async-done | bytes 4194320 | tf_op jit(solution)/shard_map/psum | solution.py:12
  171.4 12.2 fusion.89
  183.9 3.9 select_bitcast_fusion
  187.8 27.2 %all-reduce.10.cloned.1.call-done = f32[256,256]{0,1:T(8,128)} async-done(((f32[256,256]{0,1:T(8,128)}), f32[256,256]{0,1:T(8,128)}) %all-reduce.10.cloned.1.call-update) | async-done | bytes 262160 | tf_op jit(solution)/shard_map/psum | solution.py:75
  217.1 11.7 cholesky.50
  228.9 9.8 custom-call.78
  239.2 11.7 cholesky.105
  253.0 4.0 while.404
  257.0 20.1 custom-call.96
  277.1 3.7 fusion.92
  280.8 4.8 convolution_subtract_fusion.2
  287.4 3.5 fusion.110
  303.6 22.2 %all-reduce.12.cloned.1.call-done = f32[256,256]{1,0:T(8,128)} async-done(((f32[256,256]{1,0:T(8,128)}), f32[256,256]{1,0:T(8,128)}) %all-reduce.12.cloned.1.call-update) | async-done | bytes 262160 | tf_op jit(solution)/shard_map/psum | solution.py:12
  326.7 37.3 %while.388 = (s32[]{:T(128)}, f32[256,16]{0,1:T(8,128)S(1)}, f32[256]{0:T(256)S(1)}, s32[]{:T(128)}, s32[]{:T(128)}, /*index=5*/s32[]{:T(128)}, s32[]{:T(128)}, f32[]{:T(128)}, f32[]{:T(128)}, f32[]{:T(128)}) while((s32[]{:T(128)}, f32[256,16]{0,1:T(8,128)S(1)}, f32[256]{0:T(256)S(1)}, s32[]{:T(128)}, s32[]{:T(128)}, ...), condition=%wide.region_9.11_spmd.clone.clone, body=%wide.region_8.10_spmd.clone.clone.sunk | while | flops 9771 | bytes 75177 | solution.py:46
  368.7 3.0 dynamic-slice_select_fusion.1
  373.1 3.6 scatter.220
  376.7 2.4 scatter.221
  380.2 37.4 %while.389 = (s32[]{:T(128)}, f32[256,16]{0,1:T(8,128)S(1)}, f32[256]{0:T(256)S(1)}, s32[]{:T(128)}, s32[]{:T(128)}, /*index=5*/s32[]{:T(128)}, s32[]{:T(128)}, ...) while((s32[]{:T(128)}, f32[256,16]{0,1:T(8,128)S(1)}, ...), condition=%wide.region_13.15_spmd.clone.clone, body=%wide.region_12.14_spmd.clone.clone.sunk | while | flops 9775 | bytes 74223 | solution.py:46
  424.8 2.3 scatter.225
  427.1 2.4 scatter.226
  430.5 37.4 %while.390 = (s32[]{:T(128)}, f32[256,16]{0,1:T(8,128)S(1)}, f32[256]{0:T(256)S(1)}, s32[]{:T(128)}, s32[]{:T(128)}, /*index=5*/s32[]{:T(128)}, s32[]{:T(128)}, ...) while((s32[]{:T(128)}, f32[256,16]{0,1:T(8,128)S(1)}, ...), condition=%wide.region_16.18_spmd.clone.clone, body=%wide.region_15.17_spmd.clone.clone.sunk | while | flops 9775 | bytes 74223 | solution.py:46
  475.2 2.2 scatter.230
  477.5 2.3 scatter.231
  480.9 37.4 %while.391 = (s32[]{:T(128)}, f32[256,16]{0,1:T(8,128)S(1)}, f32[256]{0:T(256)S(1)}, s32[]{:T(128)}, s32[]{:T(128)}, /*index=5*/s32[]{:T(128)}, s32[]{:T(128)}, ...) while((s32[]{:T(128)}, f32[256,16]{0,1:T(8,128)S(1)}, ...), condition=%wide.region_19.21_spmd.clone.clone, body=%wide.region_18.20_spmd.clone.clone.sunk | while | flops 9775 | bytes 74223 | solution.py:46
  525.6 2.2 scatter.235
  527.8 2.3 scatter.237
  531.2 37.4 %while.392 = (s32[]{:T(128)}, f32[256,16]{0,1:T(8,128)S(1)}, f32[256]{0:T(256)S(1)}, s32[]{:T(128)}, s32[]{:T(128)}, /*index=5*/s32[]{:T(128)}, s32[]{:T(128)}, ...) while((s32[]{:T(128)}, f32[256,16]{0,1:T(8,128)S(1)}, ...), condition=%wide.region_22.24_spmd.clone.clone, body=%wide.region_21.23_spmd.clone.clone.sunk | while | flops 9775 | bytes 74223 | solution.py:46
  575.9 2.3 scatter.241
  581.4 37.4 %while.393 = (s32[]{:T(128)}, f32[256,16]{0,1:T(8,128)S(1)}, f32[256]{0:T(256)S(1)}, s32[]{:T(128)}, s32[]{:T(128)}, /*index=5*/s32[]{:T(128)}, s32[]{:T(128)}, ...) while((s32[]{:T(128)}, f32[256,16]{0,1:T(8,128)S(1)}, ...), condition=%wide.region_25.27_spmd.clone.clone, body=%wide.region_24.26_spmd.clone.clone.sunk | while | flops 9775 | bytes 74223 | solution.py:46
  626.0 2.2 scatter.246
  631.5 37.4 %while.394 = (s32[]{:T(128)}, f32[256,16]{0,1:T(8,128)S(1)}, f32[256]{0:T(256)S(1)}, s32[]{:T(128)}, s32[]{:T(128)}, /*index=5*/s32[]{:T(128)}, s32[]{:T(128)}, ...) while((s32[]{:T(128)}, f32[256,16]{0,1:T(8,128)S(1)}, ...), condition=%wide.region_28.30_spmd.clone.clone, body=%wide.region_27.29_spmd.clone.clone.sunk | while | flops 9775 | bytes 74223 | solution.py:46
  676.2 2.5 scatter.251
  681.9 37.4 %while.395 = (s32[]{:T(128)}, f32[256,16]{0,1:T(8,128)S(1)}, f32[256]{0:T(256)S(1)}, s32[]{:T(128)}, s32[]{:T(128)}, /*index=5*/s32[]{:T(128)}, s32[]{:T(128)}, ...) while((s32[]{:T(128)}, f32[256,16]{0,1:T(8,128)S(1)}, ...), condition=%wide.region_31.33_spmd.clone.clone, body=%wide.region_30.32_spmd.clone.clone.sunk | while | flops 9775 | bytes 74223 | solution.py:46
  727.2 37.4 %while.396 = (s32[]{:T(128)}, f32[256,16]{0,1:T(8,128)S(1)}, f32[256]{0:T(256)S(1)}, s32[]{:T(128)}, s32[]{:T(128)}, /*index=5*/s32[]{:T(128)}, s32[]{:T(128)}, ...) while((s32[]{:T(128)}, f32[256,16]{0,1:T(8,128)S(1)}, ...), condition=%wide.region_34.36_spmd.clone.clone, body=%wide.region_33.35_spmd.clone.clone.sunk | while | flops 9775 | bytes 74223 | solution.py:46
  770.1 37.4 %while.397 = (s32[]{:T(128)}, f32[256,16]{0,1:T(8,128)S(1)}, f32[256]{0:T(256)S(1)}, s32[]{:T(128)}, s32[]{:T(128)}, /*index=5*/s32[]{:T(128)}, s32[]{:T(128)}, ...) while((s32[]{:T(128)}, f32[256,16]{0,1:T(8,128)S(1)}, ...), condition=%wide.region_37.39_spmd.clone.clone, body=%wide.region_36.38_spmd.clone.clone.sunk | while | flops 9775 | bytes 74223 | solution.py:46
  813.3 37.4 %while.398 = (s32[]{:T(128)}, f32[256,16]{0,1:T(8,128)S(1)}, f32[256]{0:T(256)S(1)}, s32[]{:T(128)}, s32[]{:T(128)}, /*index=5*/s32[]{:T(128)}, s32[]{:T(128)}, ...) while((s32[]{:T(128)}, f32[256,16]{0,1:T(8,128)S(1)}, ...), condition=%wide.region_40.42_spmd.clone.clone, body=%wide.region_39.41_spmd.clone.clone.sunk | while | flops 9775 | bytes 74223 | solution.py:46
  856.3 37.4 %while.399 = (s32[]{:T(128)}, f32[256,16]{0,1:T(8,128)S(1)}, f32[256]{0:T(256)S(1)}, s32[]{:T(128)}, s32[]{:T(128)}, /*index=5*/s32[]{:T(128)}, s32[]{:T(128)}, ...) while((s32[]{:T(128)}, f32[256,16]{0,1:T(8,128)S(1)}, ...), condition=%wide.region_43.45_spmd.clone.clone, body=%wide.region_42.44_spmd.clone.clone.sunk | while | flops 9775 | bytes 74223 | solution.py:46
  899.3 37.4 %while.400 = (s32[]{:T(128)}, f32[256,16]{0,1:T(8,128)S(1)}, f32[256]{0:T(256)S(1)}, s32[]{:T(128)}, s32[]{:T(128)}, /*index=5*/s32[]{:T(128)}, s32[]{:T(128)}, ...) while((s32[]{:T(128)}, f32[256,16]{0,1:T(8,128)S(1)}, ...), condition=%wide.region_46.48_spmd.clone.clone, body=%wide.region_45.47_spmd.clone.clone.sunk | while | flops 9775 | bytes 74223 | solution.py:46
  942.2 37.4 %while.401 = (s32[]{:T(128)}, f32[256,16]{0,1:T(8,128)S(1)}, f32[256]{0:T(256)S(1)}, s32[]{:T(128)}, s32[]{:T(128)}, /*index=5*/s32[]{:T(128)}, s32[]{:T(128)}, ...) while((s32[]{:T(128)}, f32[256,16]{0,1:T(8,128)S(1)}, ...), condition=%wide.region_49.51_spmd.clone.clone, body=%wide.region_48.50_spmd.clone.clone.sunk | while | flops 9775 | bytes 74223 | solution.py:46
  985.5 37.4 %while.402 = (s32[]{:T(128)}, f32[256,16]{0,1:T(8,128)S(1)}, f32[256]{0:T(256)S(1)}, s32[]{:T(128)}, s32[]{:T(128)}, /*index=5*/s32[]{:T(128)}, s32[]{:T(128)}, ...) while((s32[]{:T(128)}, f32[256,16]{0,1:T(8,128)S(1)}, ...), condition=%wide.region_52.54_spmd.clone.clone, body=%wide.region_51.53_spmd.clone.clone.sunk | while | flops 9775 | bytes 74223 | solution.py:46
  1028.2 37.4 %while.403 = (s32[]{:T(128)}, f32[256,16]{0,1:T(8,128)S(1)}, f32[256]{0:T(256)S(1)}, s32[]{:T(128)}, s32[]{:T(128)}, /*index=5*/s32[]{:T(128)}, s32[]{:T(128)}, ...) while((s32[]{:T(128)}, f32[256,16]{0,1:T(8,128)S(1)}, ...), condition=%wide.region_54.56_spmd.clone.clone, body=%wide.region_53.55_spmd.clone.clone.sunk | while | flops 9775 | bytes 74223 | solution.py:46
  1066.8 4.2 while.405
  1071.0 19.8 custom-call.97
  1092.8 3.4 convolution_subtract_fusion.1
  1096.3 3.3 fusion.107
  1099.7 16.1 gather_fusion
  1115.8 5.8 copy.109
  1121.7 3.8 fusion.85
  1129.1 4.2 while.387
  1133.3 19.7 custom-call.94
  1154.1 26.6 %all-reduce.14.cloned.1.call-done = f32[2048,256]{0,1:T(8,128)} async-done(((f32[2048,256]{0,1:T(8,128)}), f32[2048,256]{0,1:T(8,128)}) %all-reduce.14.cloned.1.call-update) | async-done | bytes 2097168 | tf_op jit(solution)/shard_map/psum | solution.py:12
  1180.7 5.0 fusion.101
  1185.7 58.5 %convolution_bitcast_fusion = f32[4096,256]{0,1:T(8,128)} fusion(f32[2048,256]{1,0:T(8,128)S(1)} %fusion.101, f32[4096,2048]{1,0:T(8,128)} %param.159), kind=kOutput, calls=%fused_computation.206 | convolution fusion | flops 25769803776 | bytes 39845888 | tf_op jit(solution)/shard_map/dot_general | solution.py:16
  1244.3 8.5 fusion.99
  1252.8 33.3 %convolution_bitcast_fusion.1 = f32[2048,256]{0,1:T(8,128)} fusion(f32[4096,256]{1,0:T(8,128)S(1)} %fusion.99, f32[4096,2048]{1,0:T(8,128)} %param.159), kind=kOutput, calls=%fused_computation.222 | convolution fusion | flops 25769803776 | bytes 39845888 | tf_op jit(solution)/shard_map/dot_general | solution.py:16
  1286.2 596.0 %all-gather.3.cloned.1.call-done = f32[32768,256]{0,1:T(8,128)} async-done(((f32[4096,256]{0,1:T(8,128)}), f32[32768,256]{0,1:T(8,128)}) %all-gather.3.cloned.1.call-update) | async-done | bytes 33554448 | tf_op jit(solution)/shard_map/all_gather | solution.py:91
  1882.1 28.9 %copy.131 = f32[32,8,8,4096]{3,2,1,0:T(8,128)S(1)} copy(f32[32,8,8,4096]{3,1,2,0:T(8,128)} %bitcast.551) | data formatting | bytes 67108864
  1911.1 12.7 bitcast_reduce_fusion
  1923.7 7.7 fusion.222
  1933.5 53.7 %all-reduce.16.cloned.1.call-done = (f32[256,256]{1,0:T(8,128)}, f32[2048,256]{0,1:T(8,128)}) async-done(((f32[256,256]{1,0:T(8,128)}, f32[2048,256]{0,1:T(8,128)}), (f32[256,256]{1,0:T(8,128)}, f32[2048,256]{0,1:T(8,128)})) %all-reduce.16.cloned.1.call-update) | async-done | bytes 2359312 | tf_op jit(solution)/shard_map/psum | solution.py:92
  1988.6 8.4 fusion.83
  2000.0 3.9 fusion.91
  2003.9 59.6 %convolution_subtract_fusion = f32[4096,2048]{1,0:T(8,128)} fusion(f32[4096,2048]{1,0:T(8,128)} %param.159, f32[4096,256]{0,1:T(8,128)} %copy-done.2, f32[4096,256]{0,1:T(8,128)S(1)} %copy-done.1, f32[2048,256]{0,1:T(8,128)S(1)} %copy-done.7, f32[2048,256]{0,1:T(8,128)S(1)} %fusion.91), kind=kOutput, calls=%fused_computation.200 | convolution fusion | flops 51551141888 | bytes 79691776 | tf_op jit(solution)/shard_map/dot_general | solution.py:16
  (2317 shorter events, 410.0 us)
Async XLA Ops:
  7.2 164.2 %all-reduce.8.cloned.1.call-start = ((), (), s32[]{:S(2)}) async-start(), calls=%async_computation | async-start | bytes 8388608 | tf_op jit(solution)/shard_map/psum | solution.py:12
  11.7 203.3 %all-reduce.10.cloned.1.call-start = ((), (), s32[]{:S(2)}) async-start(), calls=%async_computation.1 | async-start | bytes 524288 | tf_op jit(solution)/shard_map/psum | solution.py:75
  183.6 142.1 %all-reduce.12.cloned.1.call-start = ((), (), s32[]{:S(2)}) async-start(), calls=%async_computation.2 | async-start | bytes 524288 | tf_op jit(solution)/shard_map/psum | solution.py:12
  277.1 3.7 copy-start.8
  287.4 4.9 copy-start.9
  290.9 1.3 copy-start.5
  292.3 10.6 copy-start.10
  293.3 887.4 %all-reduce.14.cloned.1.call-start = ((), (), s32[]{:S(2)}) async-start(), calls=%async_computation.3 | async-start | bytes 4194304 | tf_op jit(solution)/shard_map/psum | solution.py:12
  1090.8 2.0 copy-start.6
  1092.8 6.8 copy-start.3
  1115.8 5.8 copy-start.4
  1125.4 2.1 copy-start
  1129.0 753.1 %all-gather.3.cloned.1.call-start = ((), (), s32[]{:S(2)}) async-start(), calls=%async_computation.4 | async-start | bytes 37748736 | tf_op jit(solution)/shard_map/all_gather | solution.py:91
  1244.3 743.0 %all-reduce.16.cloned.1.call-start = ((), (), s32[]{:S(2)}) async-start(), calls=%async_computation.5 | async-start | bytes 4718592 | tf_op jit(solution)/shard_map/psum | solution.py:92
  1988.6 11.4 copy-start.7
  1997.0 2.0 copy-start.2
  2000.0 3.9 copy-start.1
Sparse Core Ops, SparseCore 0:
  12.2 159.0 all-reduce.7
  183.7 31.2 all-reduce.9
  293.4 32.2 all-reduce.11
  1129.2 51.4 all-reduce.13
  1244.4 637.7 all-gather.2
  1931.6 55.6 all-reduce.15
